TPU v7x, 512 devices: a whole 4x8x8 slice. The times are simulated.
512 devices in a mesh: tp: 8 (over y), vocab: 64 (over x, z, core).
Axes of the slice: x: 4, y: 8, z: 8, core: 2. Of those that a mesh axis runs over, the one named last changes fastest.
Arguments:
- partials: float32 [8, 1024, 8192], P('tp', 'vocab'), may hold values from -2.5 to 2.5
- residual: bfloat16 [1024, 8192], P('vocab', 'tp'), may hold values from -16 to 16
- norm_gain: float32 [8192], P('tp'), may hold values from 0.5 to 1.5
- head_weight: bfloat16 [8192, 98304], P('tp', 'vocab'), may hold values from -8 to 8
- owners: int32 [1024], P('tp'), may hold values from 0 to 63, as said below
- allowed: int32 [1024, 256], P('tp'), may hold values from 0 to 768, as said below
- counts: int32 [1024], P('tp'), may hold values from 1 to 256, as said below
Outputs:
- allowed_logprobs: float32 [2048, 256, 128], P(('tp', 'vocab'))
Inputs may be any that keep to these rules, and one draw needn't show every extreme that they name: `owners`: within each group of 128 consecutive rows no owner has more than 4 rows, and one owner has exactly 4. `allowed`: block b holds vocabulary ids 128 * b to 128 * b + 127. The first counts[r] entries of a row are distinct and ascending, the rest equal 768; at most 4 of a row's blocks lie among blocks 12 * v to 12 * v + 11 for any v, and in each group of rows the rows of one owner reach 4 for every v. `counts`: each group of 128 consecutive rows has a row with 256.
All inputs are finite; a program needn't handle non-finite values.
Results may differ from a plain program's by a relative error of at most 0.00032.
Values sent between devices are 32-bit elements; how exact they have to be, the bound alone decides.
A program may use at most 64 MiB of HBM per device.

v0:
```python
import jax
import jax.numpy as jnp
from jax import lax
from jax.sharding import PartitionSpec as P

EPSILON = 1e-05


def combined_all(shard, axis, combine):
    everything = jax.tree.map(lambda part: lax.all_gather(part, axis), shard)
    first = jax.tree.map(lambda part: part[0], everything)

    def turn(k, so_far):
        return combine(so_far, jax.tree.map(lambda part: part[k], everything))

    return lax.fori_loop(1, lax.axis_size(axis), turn, first)


def slot_ranks(owners):
    row_order = jnp.arange(owners.shape[0], dtype=jnp.int32)
    same_owner = (owners[:, None] == owners[None, :]) & (row_order[:, None] < row_order[None, :])
    return jnp.sum(same_owner.astype(jnp.int32), axis=0)


def combine_stats(first, second):
    larger = jnp.maximum(first[0], second[0])
    merged = first[1] * jnp.exp(first[0] - larger) + second[1] * jnp.exp(second[0] - larger)
    return (larger, merged)


def body(partials, residual, norm_gain, head_weight, owners, allowed, counts):
    tp_count = lax.axis_size("tp")
    vocab_count = lax.axis_size("vocab")
    tp_index = lax.axis_index("tp")
    vocab_index = lax.axis_index("vocab")
    summed = lax.psum_scatter(partials, "tp", scatter_dimension=2, tiled=True)[0]
    hidden_rows = summed + residual.astype(jnp.float32)
    every_row = lax.all_gather(hidden_rows, "vocab", axis=0, tiled=True)
    square_part = jnp.sum(every_row * every_row, axis=1)
    scaled = (every_row * norm_gain).astype(jnp.bfloat16)
    head_terms = jnp.dot(scaled, head_weight, preferred_element_type=jnp.float32)
    own_rows = head_terms.shape[0] // tp_count
    total_terms, total_squares = lax.psum((head_terms, square_part), "tp")
    raw_logits = lax.dynamic_slice_in_dim(total_terms, tp_index * own_rows, own_rows, 0)
    sumsq = lax.dynamic_slice_in_dim(total_squares, tp_index * own_rows, own_rows, 0)
    width = head_weight.shape[0] * tp_count
    logits = raw_logits * lax.rsqrt(sumsq / width + EPSILON)[:, None]
    row_top = jnp.max(logits, axis=1)
    row_total = jnp.sum(jnp.exp(logits - row_top[:, None]), axis=1)
    big_top, big_total = combined_all((row_top, row_total), "vocab", combine_stats)
    logprob = logits - (big_top + jnp.log(big_total))[:, None]
    block_width = 128
    blocks_here = logprob.shape[1] // block_width
    list_width = allowed.shape[1]
    per_owner = 2 * own_rows // vocab_count
    slot_rank = slot_ranks(owners)
    target_row = owners * per_owner + slot_rank
    slot_index = jnp.arange(per_owner, dtype=jnp.int32)[:, None]
    owned_slot = ((owners[None, :] == vocab_index) & (slot_rank[None, :] == slot_index)).astype(
        jnp.int32
    )
    slot_lists = jnp.sum(owned_slot[:, :, None] * allowed[None, :, :], axis=1)
    slot_counts = jnp.sum(owned_slot * counts[None, :], axis=1)
    slot_used = jnp.sum(owned_slot, axis=1) > 0
    positions = jnp.arange(list_width, dtype=jnp.int32)
    live_entry = (positions[None, :] < slot_counts[:, None]) & slot_used[:, None]
    source = jnp.clip(slot_lists // blocks_here, 0, vocab_count - 1)
    outgoing = (
        jnp.zeros((vocab_count * per_owner, logprob.shape[1]), jnp.float32)
        .at[target_row]
        .set(logprob)
    )
    incoming = lax.all_to_all(outgoing, "vocab", split_axis=0, concat_axis=0, tiled=True)
    local_block = jnp.clip(slot_lists - source * blocks_here, 0, blocks_here - 1)
    table_row = (source * per_owner + slot_index) * blocks_here + local_block
    received = incoming.reshape(vocab_count * per_owner * blocks_here, block_width)
    gathered = jnp.take(received, jnp.where(live_entry, table_row, 0), axis=0)
    return jnp.where(live_entry[:, :, None], gathered, 0.0)


def solution(mesh):
    placed = (
        P("tp", "vocab", None),
        P("vocab", "tp"),
        P("tp"),
        P("tp", "vocab"),
        P("tp"),
        P("tp", None),
        P("tp"),
    )
    return jax.shard_map(
        body, mesh=mesh, in_specs=placed, out_specs=P(("tp", "vocab"), None, None), check_vma=False
    )
```

profile of v0, /device:TPU:1, one launch (start us, length us, event | category | flops | bytes accessed | tf_op | source)
XLA Modules:
  0.0 454.8 jit_solution(10723882231364105710)
XLA Ops:
  6.5 0.0 copy-start
  6.5 0.0 reduce-scatter.2.cloned.1.call-start
  6.5 0.7 reduce-scatter.2.cloned.1.call-update
  7.3 0.0 all-gather.6.cloned.1.call-start
  7.3 43.3 %reduce-scatter.2.cloned.1.call-done = f32[1,16,1024]{2,1,0:T(8,128)} async-done(((f32[1,16,8192]{2,1,0:T(8,128)}), f32[1,16,1024]{2,1,0:T(8,128)}) %reduce-scatter.2.cloned.1.call-update) | async-done | bytes 65552 | tf_op jit(solution)/shard_map/reduce_scatter | solution.py:36
  50.6 1.5 bitcast_add_fusion
  52.1 0.0 all-gather.6.cloned.1.call-update
  52.1 0.0 all-reduce.2.cloned.1.call-start
  52.2 91.4 %all-gather.6.cloned.1.call-done = f32[1024,1024]{1,0:T(8,128)} async-done(((f32[16,1024]{1,0:T(8,128)}), f32[1024,1024]{1,0:T(8,128)}) %all-gather.6.cloned.1.call-update) | async-done | bytes 4194320 | tf_op jit(solution)/shard_map/all_gather | solution.py:38
  143.6 0.0 copy-done
  143.6 7.6 %fusion.2 = f32[1024,1536]{1,0:T(8,128)} fusion(bf16[1024,1536]{1,0:T(8,128)(2,1)S(1)} %copy-done, f32[1024,1024]{1,0:T(8,128)} %all-gather.6.cloned.1.call-done, f32[1024]{0:T(1024)} %param.11), kind=kOutput, calls=%fused_computation.10 | convolution fusion | flops 3223322624 | bytes 13635584 | tf_op jit(solution)/shard_map/dot_general | solution.py:41
  151.2 0.0 copy-start.3
  151.2 0.0 all-reduce.2.cloned.1.call-update
  151.3 0.6 copy-done.3
  151.9 0.1 convert_reduce_fusion
  152.0 2.5 multiply_reduce_fusion
  154.5 14.3 %psum.15 = f32[1024]{0:T(1024)S(1)} all-reduce(f32[1024]{0:T(1024)S(1)} %multiply_reduce_fusion), channel_id=1, replica_groups=mesh['tp'=8,'vocab'=64] {'tp'}, use_global_device_ids=true, to_apply=%region_7.0 | all-reduce | flops 1024 | bytes 8192 | tf_op jit(solution)/shard_map/psum | solution.py:43
  168.8 0.1 add_rsqrt_fusion
  168.9 132.2 %all-reduce.2.cloned.1.call-done = f32[1024,1536]{1,0:T(8,128)} async-done(((f32[1024,1536]{1,0:T(8,128)}), f32[1024,1536]{1,0:T(8,128)}) %all-reduce.2.cloned.1.call-update) | async-done | bytes 6291472 | tf_op jit(solution)/shard_map/psum | solution.py:43
  301.1 1.3 fusion.7
  302.4 1.4 exponential_reduce_fusion
  303.8 42.2 %all-gather.3 = f32[64,1,128]{2,1,0:T(1,128)S(1)} all-gather(f32[1,1,128]{2,1,0:T(1,128)S(1)} %bitcast.60), channel_id=3, replica_groups=mesh['tp'=8,'vocab'=64] {'vocab'}, dimensions={0}, use_global_device_ids=true | all-gather | bytes 33280 | tf_op jit(solution)/shard_map/all_gather | solution.py:10
  346.0 37.4 %all-gather.2 = f32[64,1,128]{2,1,0:T(1,128)S(1)} all-gather(f32[1,1,128]{2,1,0:T(1,128)S(1)} %bitcast.59), channel_id=2, replica_groups=mesh['tp'=8,'vocab'=64] {'vocab'}, dimensions={0}, use_global_device_ids=true | all-gather | bytes 33280 | tf_op jit(solution)/shard_map/all_gather | solution.py:10
  383.5 2.8 while.17
  386.3 3.0 scatter_custom_fusion
  389.4 0.0 copy-start.2
  389.4 0.0 copy-start.1
  389.4 2.8 all_to_all.6
  392.1 6.0 %all-to-all-start = ((f32[64,4,1536]{2,1,0:T(4,128)}), f32[64,4,1536]{2,1,0:T(4,128)}, u32[]{:S(2)}, u32[]{:S(2)}) async-start(f32[64,4,1536]{2,1,0:T(4,128)} %all_to_all.6), calls=%async_computation.1 | async-start | bytes 3145728 | tf_op jit(solution)/shard_map/all_to_all | solution.py:73
  398.2 0.0 copy-done.2
  398.2 0.1 fusion.23
  398.4 0.0 copy-done.1
  398.4 0.1 multiply_reduce_fusion.1
  398.5 0.1 fusion.11
  398.6 0.1 fusion.17
  398.7 39.2 %all-to-all-done = f32[64,4,1536]{2,1,0:T(4,128)} async-done(((f32[64,4,1536]{2,1,0:T(4,128)}), f32[64,4,1536]{2,1,0:T(4,128)}, u32[]{:S(2)}, u32[]{:S(2)}) %all-to-all-start) | async-done | bytes 1572896 | tf_op jit(solution)/shard_map/all_to_all | solution.py:73
  437.9 2.8 reshape.237
  440.7 5.4 %gather_fusion = f32[1024,128]{1,0:T(8,128)} fusion(f32[3072,128]{1,0:T(8,128)} %reshape.237, s32[1024]{0:T(1024)S(1)} %broadcast_clamp_fusion), kind=kCustom, calls=%fused_computation | custom fusion | bytes 1052672 | tf_op jit(solution)/shard_map/jit(_take)/gather | solution.py:77
  446.1 2.2 select_select_fusion
  (72 shorter events, 1.8 us)
Async XLA Ops:
  6.5 137.1 %copy-start = (bf16[1024,1536]{1,0:T(8,128)(2,1)S(1)}, bf16[1024,1536]{1,0:T(8,128)(2,1)}, u32[]{:S(2)}) copy-start(bf16[1024,1536]{1,0:T(8,128)(2,1)} %param.12) | copy-start | bytes 9437188
  6.5 44.1 %reduce-scatter.2.cloned.1.call-start = ((), (), s32[]{:S(2)}) async-start(), calls=%async_computation.2 | async-start | bytes 589824 | tf_op jit(solution)/shard_map/reduce_scatter | solution.py:36
  7.3 136.4 %all-gather.6.cloned.1.call-start = ((), (), s32[]{:S(2)}) async-start(), calls=%async_computation.3 | async-start | bytes 4259840 | tf_op jit(solution)/shard_map/all_gather | solution.py:38
  52.1 248.9 %all-reduce.2.cloned.1.call-start = ((), (), s32[]{:S(2)}) async-start(), calls=%async_computation.4 | async-start | bytes 12582912 | tf_op jit(solution)/shard_map/psum | solution.py:43
  151.2 0.7 copy-start.3
  389.4 8.8 %copy-start.2 = (s32[128]{0:T(128)S(1)}, s32[128]{0:T(128)}, u32[]{:S(2)}) copy-start(s32[128]{0:T(128)} %param.15) | copy-start | bytes 1540
  389.4 9.0 %copy-start.1 = (s32[128,256]{1,0:T(8,128)S(1)}, s32[128,256]{1,0:T(8,128)}, u32[]{:S(2)}) copy-start(s32[128,256]{1,0:T(8,128)} %param.14) | copy-start | bytes 393220
  392.1 45.8 %all-to-all-start = ((f32[64,4,1536]{2,1,0:T(4,128)}), f32[64,4,1536]{2,1,0:T(4,128)}, u32[]{:S(2)}, u32[]{:S(2)}) async-start(f32[64,4,1536]{2,1,0:T(4,128)} %all_to_all.6), calls=%async_computation.1 | async-start | bytes 3145728 | tf_op jit(solution)/shard_map/all_to_all | solution.py:73
Sparse Core Ops, SparseCore 0:
  10.1 40.4 reduce-scatter.1
  54.0 89.5 all-gather.5
  151.4 149.6 all-reduce.1
where the time goes:
time: 455 us
  waiting for transfers between devices  307 us (67%)
  blocking collectives  93.9 us (21%)
  other arithmetic  14.4 us (3%)
  between operations  13.2 us (3%)
  local copies, waits for them, and re-layouts  11.6 us (3%)
  matrix products  7.62 us (2%)
  starting transfers between devices  6.13 us (1%)
    psum x1, waiting for transfers between devices, body(): total_terms, total_squares = lax.psum((head_terms, square_part), 'tp')  132 us
    all_gather x1, waiting for transfers between devices, body(): every_row = lax.all_gather(hidden_rows, 'vocab', axis=0, tiled=True)  91.4 us
    all_gather x2, blocking collectives, combined_all(): everything = jax.tree.map(lambda part: lax.all_gather(part, axis), shard)  79.7 us
    reduce_scatter x1, waiting for transfers between devices, body(): lax.psum_scatter(partials, 'tp', scatter_dimension=2, tiled=True)[0]  43.3 us
    all_to_all x1, waiting for transfers between devices, body(): lax.all_to_all(outgoing, 'vocab', split_axis=0, concat_axis=0, tiled=True)  39.2 us
    psum x1, blocking collectives, body(): total_terms, total_squares = lax.psum((head_terms, square_part), 'tp')  14.3 us
  transfers between devices with their start and end apart: 4, of which 4 were waited for; matrix products, arithmetic and copies ran while one was open for 1% of the time, Pallas kernels for 0%

commit v1 on v0

v1 whole, which is shorter than its diff:
```python
import jax
import jax.numpy as jnp
from jax import lax
from jax.sharding import PartitionSpec as P

EPSILON = 1e-05
BLOCK = 128
KMAX = 4


def slot_ranks(owners):
    row_order = jnp.arange(owners.shape[0], dtype=jnp.int32)
    same_owner = (owners[:, None] == owners[None, :]) & (row_order[:, None] < row_order[None, :])
    return jnp.sum(same_owner.astype(jnp.int32), axis=0)


def tail(raw_logits, sumsq, width, owners, allowed, counts):
    vocab_count = lax.axis_size("vocab")
    vocab_index = lax.axis_index("vocab")
    own_rows, columns = raw_logits.shape
    blocks_here = columns // BLOCK
    list_width = allowed.shape[1]
    per_owner = 2 * own_rows // vocab_count
    positions = jnp.arange(list_width, dtype=jnp.int32)

    slot_rank = slot_ranks(owners)
    mine = jnp.where(positions[None, :] < counts[:, None], allowed, -1) - vocab_index * blocks_here
    here = jnp.arange(blocks_here, dtype=jnp.int32)
    present = jnp.any(mine[:, None, :] == here[None, :, None], axis=2).astype(jnp.int32)
    place = jnp.sum(jnp.where(here[:, None] < here[None, :], present[:, :, None], 0), axis=1)
    place = jnp.where(present > 0, place, -1)
    target_row = owners * per_owner + slot_rank
    slots = jnp.arange(vocab_count * per_owner, dtype=jnp.int32)
    to_slot = (target_row[None, :] == slots[:, None]).astype(jnp.float32)

    slot_index = jnp.arange(per_owner, dtype=jnp.int32)[:, None]
    owned_slot = ((owners[None, :] == vocab_index) & (slot_rank[None, :] == slot_index)).astype(jnp.int32)
    slot_lists = jnp.sum(owned_slot[:, :, None] * allowed[None, :, :], axis=1)
    slot_counts = jnp.sum(owned_slot * counts[None, :], axis=1)
    live_entry = positions[None, :] < slot_counts[:, None]
    source = jnp.clip(slot_lists // blocks_here, 0, vocab_count - 1)
    rank = jnp.zeros_like(source)
    for back in range(1, KMAX):
        earlier = jnp.pad(source, ((0, 0), (back, 0)), constant_values=-1)[:, :list_width]
        rank = rank + (earlier == source).astype(jnp.int32)
    table_row = (source * per_owner + slot_index) * (KMAX + 1) + jnp.minimum(rank, KMAX - 1)
    table_row = jnp.where(live_entry, table_row, 0)

    logits = raw_logits * lax.rsqrt(sumsq / width + EPSILON)[:, None]
    row_top = jnp.max(logits, axis=1)
    row_total = jnp.sum(jnp.exp(logits - row_top[:, None]), axis=1)
    picked = []
    for k in range(KMAX):
        chosen = jnp.zeros((own_rows, BLOCK), jnp.float32)
        for b in range(blocks_here):
            block = logits[:, b * BLOCK : (b + 1) * BLOCK]
            chosen = jnp.where((place[:, b] == k)[:, None], block, chosen)
        picked.append(chosen)
    lane = jnp.arange(BLOCK, dtype=jnp.int32)[None, :]
    picked.append(jnp.where(lane == 0, row_top[:, None], jnp.where(lane == 1, row_total[:, None], 0.0)))
    payload = jnp.concatenate(picked, axis=1)
    outgoing = jnp.dot(
        to_slot, payload, precision=lax.Precision.HIGHEST, preferred_element_type=jnp.float32
    ).reshape(vocab_count, per_owner, (KMAX + 1) * BLOCK)
    incoming = lax.all_to_all(outgoing, "vocab", split_axis=0, concat_axis=0, tiled=True)
    tops = incoming[:, :, KMAX * BLOCK]
    totals = incoming[:, :, KMAX * BLOCK + 1]
    big_top = jnp.max(tops, axis=0)
    big_total = jnp.sum(totals * jnp.exp(tops - big_top[None, :]), axis=0)
    shift = big_top + jnp.log(big_total)
    received = incoming.reshape(vocab_count * per_owner * (KMAX + 1), BLOCK)
    gathered = jnp.take(received, table_row, axis=0)
    return jnp.where(live_entry[:, :, None], gathered - shift[:, None, None], 0.0)


def body(partials, residual, norm_gain, head_weight, owners, allowed, counts):
    summed = lax.psum_scatter(partials, "tp", scatter_dimension=2, tiled=True)[0]
    hidden_rows = summed + residual.astype(jnp.float32)
    every_row = lax.all_gather(hidden_rows, "vocab", axis=0, tiled=True)
    square_part = jnp.sum(every_row * every_row, axis=1)
    scaled = (every_row * norm_gain).astype(jnp.bfloat16)
    head_terms = jnp.dot(scaled, head_weight, preferred_element_type=jnp.float32)
    raw_logits = lax.psum_scatter(head_terms, "tp", scatter_dimension=0, tiled=True)
    sumsq = lax.psum_scatter(square_part, "tp", scatter_dimension=0, tiled=True)
    width = head_weight.shape[0] * lax.axis_size("tp")
    return tail(raw_logits, sumsq, width, owners, allowed, counts)


def solution(mesh):
    placed = (
        P("tp", "vocab", None),
        P("vocab", "tp"),
        P("tp"),
        P("tp", "vocab"),
        P("tp"),
        P("tp", None),
        P("tp"),
    )
    return jax.shard_map(
        body, mesh=mesh, in_specs=placed, out_specs=P(("tp", "vocab"), None, None), check_vma=False
    )
```

time: 455 us -> 281 us (0.62)
  waiting for transfers between devices: 307 us -> 208 us
  blocking collectives: 93.9 us -> 14.9 us
  starting transfers between devices: 6.13 us -> 11.2 us
    psum x1 -> x0, waiting for transfers between devices: 132 us -> none  [body(): total_terms, total_squares = lax.psum((head_terms, square_part), 'tp')]
    all_gather x2 -> x0, blocking collectives: 79.7 us -> none  [combined_all(): everything = jax.tree.map(lambda part: lax.all_gather(part, axis), shard)]
    reduce_scatter x0 -> x1, waiting for transfers between devices: none -> 53.1 us  [body(): lax.psum_scatter(head_terms, 'tp', scatter_dimension=0, tiled=True)]
    all_to_all x1, waiting for transfers between devices: 39.2 us -> 19.6 us  [tail(): lax.all_to_all(outgoing, 'vocab', split_axis=0, concat_axis=0, tiled=True)]
    unnamed x0 -> x1, blocking collectives: none -> 14.9 us
    psum x1 -> x0, blocking collectives: 14.3 us -> none  [body(): total_terms, total_squares = lax.psum((head_terms, square_part), 'tp')]
    all_to_all x1, starting transfers between devices: 6.05 us -> 11.1 us  [tail(): lax.all_to_all(outgoing, 'vocab', split_axis=0, concat_axis=0, tiled=True)]
  transfers between devices with their start and end apart: 4 -> 4, of which waited for: 4 -> 4; matrix products, arithmetic and copies ran while one was open for 1% -> 2% of each run, Pallas kernels for 0% -> 0%
where the time goes in v1:
time: 281 us; the launch traced here: 280 us
  waiting for transfers between devices  208 us (74%)
  blocking collectives  14.9 us (5%)
  between operations  14 us (5%)
  local copies, waits for them, and re-layouts  11.8 us (4%)
  other arithmetic  11.5 us (4%)
  starting transfers between devices  11.2 us (4%)
  matrix products  8.81 us (3%)
    all_gather x1, waiting for transfers between devices, body(): every_row = lax.all_gather(hidden_rows, 'vocab', axis=0, tiled=True)  91.4 us
    reduce_scatter x1, waiting for transfers between devices, body(): lax.psum_scatter(head_terms, 'tp', scatter_dimension=0, tiled=True)  53.1 us
    reduce_scatter x1, waiting for transfers between devices, body(): lax.psum_scatter(partials, 'tp', scatter_dimension=2, tiled=True)[0]  43.3 us
    all_to_all x1, waiting for transfers between devices, tail(): lax.all_to_all(outgoing, 'vocab', split_axis=0, concat_axis=0, tiled=True)  19.6 us
    unnamed x1, blocking collectives  14.9 us
    all_to_all x1, starting transfers between devices, tail(): lax.all_to_all(outgoing, 'vocab', split_axis=0, concat_axis=0, tiled=True)  11.1 us
    dot_general x1, matrix products, body(): jnp.dot(scaled, head_weight, preferred_element_type=jnp.float32)  7.54 us
  transfers between devices with their start and end apart: 4, of which 4 were waited for; matrix products, arithmetic and copies ran while one was open for 2% of the time, Pallas kernels for 0%

profile of v1, /device:TPU:1, one launch (start us, length us, event | category | flops | bytes accessed | tf_op | source)
XLA Modules:
  0.0 280.3 jit_solution(17336991937507651582)
XLA Ops:
  6.5 0.0 copy-start
  6.5 0.0 reduce-scatter.3.cloned.1.call-start
  6.5 0.7 reduce-scatter.3.cloned.1.call-update
  7.3 0.0 all-gather.2.cloned.1.call-start
  7.3 43.3 %reduce-scatter.3.cloned.1.call-done = f32[1,16,1024]{2,1,0:T(8,128)} async-done(((f32[1,16,8192]{2,1,0:T(8,128)}), f32[1,16,1024]{2,1,0:T(8,128)}) %reduce-scatter.3.cloned.1.call-update) | async-done | bytes 65552 | tf_op jit(solution)/shard_map/reduce_scatter | solution.py:77
  50.6 1.5 bitcast_add_fusion
  52.1 0.0 all-gather.2.cloned.1.call-update
  52.1 0.0 reduce-scatter.5.cloned.1.call-start
  52.2 91.4 %all-gather.2.cloned.1.call-done = f32[1024,1024]{1,0:T(8,128)} async-done(((f32[16,1024]{1,0:T(8,128)}), f32[1024,1024]{1,0:T(8,128)}) %all-gather.2.cloned.1.call-update) | async-done | bytes 4194320 | tf_op jit(solution)/shard_map/all_gather | solution.py:79
  143.6 0.0 copy-done
  143.6 7.5 %fusion = f32[1024,1536]{1,0:T(8,128)} fusion(bf16[1024,1536]{1,0:T(8,128)(2,1)S(1)} %copy-done, f32[1024,1024]{1,0:T(8,128)} %all-gather.2.cloned.1.call-done, f32[1024]{0:T(1024)} %param.9), kind=kOutput, calls=%fused_computation.3 | convolution fusion | flops 3223322624 | bytes 13635584 | tf_op jit(solution)/shard_map/dot_general | solution.py:82
  151.2 0.0 copy-start.1
  151.2 0.0 copy-start.2
  151.2 0.0 copy-start.3
  151.2 0.0 reduce-scatter.5.cloned.1.call-update
  151.2 0.9 copy-done.1
  152.1 0.0 copy-done.2
  152.1 0.1 select_subtract_fusion
  152.2 0.3 fusion.2
  152.5 1.3 dynamic-slice
  154.4 0.0 copy-done.3
  154.4 0.1 convert_reduce_fusion
  154.5 0.1 select_reduce_fusion
  154.7 2.5 multiply_reduce_fusion
  157.3 14.9 %all-reduce.3 = f32[1024]{0:T(1024)S(1)} all-reduce(f32[1024]{0:T(1024)S(1)} %multiply_reduce_fusion), channel_id=4, replica_groups=mesh['tp'=8,'vocab'=64] {'tp'}, use_global_device_ids=true, to_apply=%region_8.9.clone | all-reduce | flops 1024 | bytes 8192
  172.1 0.1 fusion.17
  172.2 53.1 %reduce-scatter.5.cloned.1.call-done = f32[128,1536]{1,0:T(8,128)} async-done(((f32[1024,1536]{1,0:T(8,128)}), f32[128,1536]{1,0:T(8,128)}) %reduce-scatter.5.cloned.1.call-update) | async-done | bytes 786448 | tf_op jit(solution)/shard_map/reduce_scatter | solution.py:83
  225.3 1.3 fusion.18
  226.6 0.3 exponential_reduce_fusion
  226.9 0.3 select_dynamic-update-slice_fusion.4
  227.2 0.3 select_dynamic-update-slice_fusion.3
  227.4 0.3 select_dynamic-update-slice_fusion.2
  227.7 0.3 select_dynamic-update-slice_fusion.1
  228.0 0.1 select_dynamic-update-slice_fusion
  228.1 1.3 fusion.3
  229.4 2.1 reshape.93
  231.5 11.1 %all-to-all-start = ((f32[64,4,640]{2,1,0:T(4,128)}), f32[64,4,640]{2,1,0:T(4,128)}, u32[]{:S(2)}, u32[]{:S(2)}) async-start(f32[64,4,640]{2,1,0:T(4,128)} %reshape.93), calls=%async_computation.2 | async-start | bytes 1310720 | tf_op jit(solution)/shard_map/all_to_all | solution.py:65
  242.6 0.1 select_reduce_fusion.1
  242.8 0.2 multiply_reduce_fusion.1
  242.9 0.1 compare_and_fusion
  243.0 19.6 %all-to-all-done = f32[64,4,640]{2,1,0:T(4,128)} async-done(((f32[64,4,640]{2,1,0:T(4,128)}), f32[64,4,640]{2,1,0:T(4,128)}, u32[]{:S(2)}, u32[]{:S(2)}) %all-to-all-start) | async-done | bytes 655392 | tf_op jit(solution)/shard_map/all_to_all | solution.py:65
  262.7 1.2 fusion.19
  263.9 0.1 copy.17
  264.0 0.1 copy.18
  264.1 0.2 fusion.13
  264.3 2.2 reshape.94
  266.5 5.1 %gather_fusion = f32[1024,128]{1,0:T(8,128)} fusion(f32[1280,128]{1,0:T(8,128)} %reshape.94, s32[1024]{0:T(1024)S(1)} %broadcast_clamp_fusion), kind=kCustom, calls=%fused_computation | custom fusion | bytes 1052672 | tf_op jit(solution)/shard_map/jit(_take)/gather | solution.py:72
  271.6 2.2 subtract_select_fusion
  (14 shorter events, 0.1 us)
Async XLA Ops:
  6.5 137.1 %copy-start = (bf16[1024,1536]{1,0:T(8,128)(2,1)S(1)}, bf16[1024,1536]{1,0:T(8,128)(2,1)}, u32[]{:S(2)}) copy-start(bf16[1024,1536]{1,0:T(8,128)(2,1)} %param.10) | copy-start | bytes 9437188
  6.5 44.1 %reduce-scatter.3.cloned.1.call-start = ((), (), s32[]{:S(2)}) async-start(), calls=%async_computation.3 | async-start | bytes 589824 | tf_op jit(solution)/shard_map/reduce_scatter | solution.py:77
  7.3 136.4 %all-gather.2.cloned.1.call-start = ((), (), s32[]{:S(2)}) async-start(), calls=%async_computation.4 | async-start | bytes 4259840 | tf_op jit(solution)/shard_map/all_gather | solution.py:79
  52.1 173.1 %reduce-scatter.5.cloned.1.call-start = ((), (), s32[]{:S(2)}) async-start(), calls=%async_computation.5 | async-start | bytes 7077888 | tf_op jit(solution)/shard_map/reduce_scatter | solution.py:83
  151.2 0.9 copy-start.1
  151.2 0.9 copy-start.2
  151.2 3.2 %copy-start.3 = (s32[128]{0:T(128)S(1)}, s32[128]{0:T(128)}, u32[]{:S(2)}) copy-start(s32[128]{0:T(128)} %param.11) | copy-start | bytes 1540
  231.5 31.2 %all-to-all-start = ((f32[64,4,640]{2,1,0:T(4,128)}), f32[64,4,640]{2,1,0:T(4,128)}, u32[]{:S(2)}, u32[]{:S(2)}) async-start(f32[64,4,640]{2,1,0:T(4,128)} %reshape.93), calls=%async_computation.2 | async-start | bytes 1310720 | tf_op jit(solution)/shard_map/all_to_all | solution.py:65
Sparse Core Ops, SparseCore 0:
  10.1 40.4 reduce-scatter.2
  54.0 89.5 all-gather.1
  151.3 73.9 reduce-scatter.4

commit v2 on v1

--- a/solution.py
+++ b/solution.py
@@ -1,6 +1,8 @@
 import jax
 import jax.numpy as jnp
 from jax import lax
+from jax.experimental import pallas as pl
+from jax.experimental.pallas import tpu as pltpu
 from jax.sharding import PartitionSpec as P
 
 EPSILON = 1e-05
@@ -73,15 +75,270 @@
     return jnp.where(live_entry[:, :, None], gathered - shift[:, None, None], 0.0)
 
 
+N_Y, N_X, N_Z = 8, 4, 8
+SUBS = 3
+
+
+def head_kernel(
+    part_ref, res_ref, gain_ref, w_hbm, raw_ref, sq_ref,
+    w, rs_in, rows, scaled, col, sq_part, sq_in, ring, term,
+    w_sem, rs_s, rs_r, ag_s, ag_r, ring_s, ring_r, sq_s, sq_r,
+):
+    y = lax.axis_index("tp")
+    v = lax.axis_index("vocab")
+    core = lax.rem(v, 2)
+    z = lax.rem(lax.div(v, 2), N_Z)
+    x = lax.div(v, 2 * N_Z)
+    turn = 1 - 2 * core
+    local_rows, share = res_ref.shape
+    half = share // 2
+    group = N_Y * local_rows
+
+    def at_x(q):
+        return lax.rem(x - turn * q + N_X, N_X)
+
+    def at_z(p):
+        return lax.rem(z - turn * p + N_Z, N_Z)
+
+    def device(p, q, c):
+        return (y, (at_x(q) * N_Z + at_z(p)) * 2 + c)
+
+    def along_tp(d):
+        return (lax.rem(y + d + N_Y, N_Y), v)
+
+    weight_copy = pltpu.make_async_copy(w_hbm, w, w_sem)
+    weight_copy.start()
+
+    peers = [along_tp(d) for d in range(1, N_Y)]
+    peers += [device(-1, 0, core), device(1, 0, core), device(0, -1, core), device(0, 1, core)]
+    peers += [device(0, 0, 1 - core)]
+    barrier = pltpu.get_barrier_semaphore()
+    for peer in peers:
+        pl.semaphore_signal(barrier, inc=1, device_id=peer, device_id_type=pl.DeviceIdType.MESH)
+    pl.semaphore_wait(barrier, len(peers))
+
+    def remote(src, dst, send_sem, recv_sem, peer):
+        return pltpu.make_async_remote_copy(
+            src_ref=src, dst_ref=dst, send_sem=send_sem, recv_sem=recv_sem,
+            device_id=peer, device_id_type=pl.DeviceIdType.MESH,
+        )
+
+    first = []
+    for d in (1, 7, 2, 6, 3, 5, 4):
+        to = lax.rem(y + d, N_Y)
+        source = part_ref.at[0, :, pl.ds(pl.multiple_of(to * share, share), share)]
+        copy = remote(source, rs_in.at[d - 1], rs_s.at[d - 1], rs_r.at[d - 1], along_tp(d))
+        copy.start()
+        first.append(copy)
+    mixed = part_ref[0, :, pl.ds(pl.multiple_of(y * share, share), share)]
+    mixed = mixed + res_ref[...].astype(jnp.float32)
+    for copy in first:
+        copy.wait_recv()
+    for d in range(1, N_Y):
+        mixed = mixed + rs_in[d - 1]
+    own = x * N_Z + z
+    rows[0, core, own] = mixed[:, :half]
+    rows[1, core, own] = mixed[:, half:]
+
+    limits = {"z": (N_Z // 2, N_Z // 2 - 1), "x": (N_X // 2, N_X // 2 - 1)}
+    places = [
+        (h, p, q)
+        for h in range(2)
+        for p in range(-limits["z"][1], limits["z"][0] + 1)
+        for q in range(-limits["x"][1], limits["x"][0] + 1)
+    ]
+    ids = {place: i for i, place in enumerate(places)}
+    sent = []
+
+    def held(h, p, q):
+        return rows.at[h, core, at_x(q) * N_Z + at_z(p)]
+
+    def pass_on(h, p, q, new_p, new_q):
+        peer = device(p - new_p, q - new_q, core)
+        i = ids[(h, new_p, new_q)]
+        copy = remote(held(h, p, q), held(h, p, q), ag_s.at[0, i], ag_r.at[0, i], peer)
+        copy.start()
+        sent.append(copy)
+
+    def to_sibling(h, p, q):
+        i = ids[(h, p, q)]
+        copy = remote(
+            held(h, p, q), held(h, p, q), ag_s.at[1, i], ag_r.at[1, i], device(0, 0, 1 - core)
+        )
+        copy.start()
+        sent.append(copy)
+
+    def along_z(h, p, q):
+        if 0 <= p < limits["z"][0]:
+            pass_on(h, p, q, p + 1, q)
+        if -limits["z"][1] < p <= 0:
+            pass_on(h, p, q, p - 1, q)
+
+    def along_x(h, p, q):
+        if 0 <= q < limits["x"][0]:
+            pass_on(h, p, q, p, q + 1)
+        if -limits["x"][1] < q <= 0:
+            pass_on(h, p, q, p, q - 1)
+
+    def arrived(h, p, q):
+        if h == 0:
+            if q == 0:
+                along_z(h, p, q)
+            along_x(h, p, q)
+        else:
+            if p == 0:
+                along_x(h, p, q)
+            along_z(h, p, q)
+        to_sibling(h, p, q)
+
+    def order(place):
+        h, p, q = place
+        main, other = (p, q) if h == 0 else (q, p)
+        return (abs(p) + abs(q), abs(other), h, main)
+
+    for h, p, q in sorted(places, key=order):
+        if (p, q) != (0, 0):
+            i = ids[(h, p, q)]
+            block = held(h, p, q)
+            remote(block, block, ag_s.at[0, i], ag_r.at[0, i], device(0, 0, 1 - core)).wait_recv()
+        arrived(h, p, q)
+    for h, p, q in sorted(places, key=order):
+        i = ids[(h, p, q)]
+        block = rows.at[h, 1 - core, at_x(-q) * N_Z + at_z(-p)]
+        remote(block, block, ag_s.at[1, i], ag_r.at[1, i], device(0, 0, 1 - core)).wait_recv()
+
+    def prepare(g):
+        for b in range(N_Y):
+            at = lax.div(g * N_Y, 2) + b // 2
+            low = rows[0, b % 2, at]
+            high = rows[1, b % 2, at]
+            start = pl.multiple_of(g * group + b * local_rows, local_rows)
+            scaled[pl.ds(start, local_rows), :half] = (low * gain_ref[:, :half]).astype(jnp.bfloat16)
+            scaled[pl.ds(start, local_rows), half:] = (high * gain_ref[:, half:]).astype(jnp.bfloat16)
+            squares = jnp.sum(low * low + high * high, axis=1, keepdims=True)
+            col[b * local_rows : (b + 1) * local_rows, :] = jnp.broadcast_to(
+                squares, (local_rows, BLOCK)
+            )
+        sq_part[g] = jnp.transpose(col[...])[:8]
+
+    width = ring.shape[-1]
+
+    def own_term(g, way, j):
+        left = scaled[pl.ds(pl.multiple_of(g * group, group), group), :]
+        start = (way * SUBS + j) * width
+        return jnp.dot(left, w[:, start : start + width], preferred_element_type=jnp.float32)
+
+    def group_at(way, s):
+        return lax.rem(y + N_Y - 1 - s, N_Y) if way == 0 else lax.rem(y + 1 + s, N_Y)
+
+    def hop(way, s, j):
+        return remote(
+            ring.at[way, s, j], ring.at[way, s + 1, j], ring_s.at[way, s, j], ring_r.at[way, s, j],
+            along_tp(1 if way == 0 else -1),
+        )
+
+    weight_copy.wait()
+    for way in range(2):
+        prepare(group_at(way, 0))
+        for j in range(SUBS):
+            ring[way, 0, j] = own_term(group_at(way, 0), way, j)
+            hop(way, 0, j).start()
+
+    @pl.loop(2, N_Y + 1)
+    def _(k):
+        @pl.when(k != N_Y - 1)
+        def _():
+            prepare(lax.rem(y + k, N_Y))
+
+    squares_out = []
+    for d in range(1, N_Y):
+        to = lax.rem(y + d, N_Y)
+        copy = remote(sq_part.at[to], sq_in.at[d - 1], sq_s.at[d - 1], sq_r.at[d - 1], along_tp(d))
+        copy.start()
+        squares_out.append(copy)
+
+    @pl.loop(1, N_Y - 1)
+    def _(s):
+        for way in range(2):
+            for j in range(SUBS):
+                term[way, j] = own_term(group_at(way, s), way, j)
+        for j in range(SUBS):
+            for way in range(2):
+                hop(way, s - 1, j).wait_recv()
+                ring[way, s, j] = ring[way, s, j] + term[way, j]
+                hop(way, s, j).start()
+
+    for way in range(2):
+        for j in range(SUBS):
+            term[way, j] = own_term(y, way, j)
+    for copy in squares_out:
+        copy.wait_recv()
+    total = sq_part[y]
+    for d in range(1, N_Y):
+        total = total + sq_in[d - 1]
+    sq_ref[...] = total
+    for j in range(SUBS):
+        for way in range(2):
+            hop(way, N_Y - 2, j).wait_recv()
+            start = (way * SUBS + j) * width
+            raw_ref[:, start : start + width] = ring[way, N_Y - 1, j] + term[way, j]
+
+    for copy in first + sent + squares_out:
+        copy.wait_send()
+
+    @pl.loop(0, N_Y - 1)
+    def _(s):
+        for way in range(2):
+            for j in range(SUBS):
+                hop(way, s, j).wait_send()
+
+
+def head(partials, residual, norm_gain, head_weight):
+    local_rows, share = residual.shape
+    columns = head_weight.shape[1]
+    group = N_Y * local_rows
+    chips = N_X * N_Z
+    width = columns // (2 * SUBS)
+    dma = pltpu.SemaphoreType.DMA
+    f32 = jnp.float32
+    vmem = pl.BlockSpec(memory_space=pltpu.VMEM)
+    raw, squares = pl.pallas_call(
+        head_kernel,
+        out_shape=[
+            jax.ShapeDtypeStruct((group, columns), f32),
+            jax.ShapeDtypeStruct((8, BLOCK), f32),
+        ],
+        in_specs=[vmem, vmem, vmem, pl.BlockSpec(memory_space=pl.ANY)],
+        out_specs=[vmem, vmem],
+        scratch_shapes=[
+            pltpu.VMEM((share, columns), jnp.bfloat16),
+            pltpu.VMEM((N_Y - 1, local_rows, share), f32),
+            pltpu.VMEM((2, 2, chips, local_rows, share // 2), f32),
+            pltpu.VMEM((2 * chips * local_rows, share), jnp.bfloat16),
+            pltpu.VMEM((group, BLOCK), f32),
+            pltpu.VMEM((N_Y, 8, BLOCK), f32),
+            pltpu.VMEM((N_Y - 1, 8, BLOCK), f32),
+            pltpu.VMEM((2, N_Y, SUBS, group, width), f32),
+            pltpu.VMEM((2, SUBS, group, width), f32),
+            dma,
+            dma((N_Y - 1,)),
+            dma((N_Y - 1,)),
+            dma((2, 2 * chips)),
+            dma((2, 2 * chips)),
+            dma((2, N_Y - 1, SUBS)),
+            dma((2, N_Y - 1, SUBS)),
+            dma((N_Y - 1,)),
+            dma((N_Y - 1,)),
+        ],
+        compiler_params=pltpu.CompilerParams(
+            collective_id=0, has_side_effects=True, vmem_limit_bytes=48 << 20
+        ),
+    )(partials, residual, norm_gain.reshape(1, share), head_weight)
+    return raw, squares[0]
+
+
 def body(partials, residual, norm_gain, head_weight, owners, allowed, counts):
-    summed = lax.psum_scatter(partials, "tp", scatter_dimension=2, tiled=True)[0]
-    hidden_rows = summed + residual.astype(jnp.float32)
-    every_row = lax.all_gather(hidden_rows, "vocab", axis=0, tiled=True)
-    square_part = jnp.sum(every_row * every_row, axis=1)
-    scaled = (every_row * norm_gain).astype(jnp.bfloat16)
-    head_terms = jnp.dot(scaled, head_weight, preferred_element_type=jnp.float32)
-    raw_logits = lax.psum_scatter(head_terms, "tp", scatter_dimension=0, tiled=True)
-    sumsq = lax.psum_scatter(square_part, "tp", scatter_dimension=0, tiled=True)
+    raw_logits, sumsq = head(partials, residual, norm_gain, head_weight)
     width = head_weight.shape[0] * lax.axis_size("tp")
     return tail(raw_logits, sumsq, width, owners, allowed, counts)
 

time: 281 us -> 158 us (0.56)
  waiting for transfers between devices: 208 us -> 19.7 us
  Pallas kernels: 0 us -> 118 us
  blocking collectives: 14.9 us -> 0 us
  between operations: 14 us -> 0.26 us
  matrix products: 8.81 us -> 0.43 us
  other arithmetic: 11.5 us -> 5.17 us
  starting transfers between devices: 11.2 us -> 5.53 us
  local copies, waits for them, and re-layouts: 11.8 us -> 8.69 us
    pallas_call x0 -> x1, Pallas kernels: none -> 118 us  [head(): pl.pallas_call(head_kernel, out_shape=[jax.ShapeDtypeStruct((group, colum...]
    reduce_scatter x2 -> x0, waiting for transfers between devices: 96.4 us -> none  [the longest x1 53.1 us: body(): lax.psum_scatter(head_terms, 'tp', scatter_dimension=0, tiled=True)]
    all_gather x1 -> x0, waiting for transfers between devices: 91.4 us -> none  [body(): every_row = lax.all_gather(hidden_rows, 'vocab', axis=0, tiled=True)]
    unnamed x1 -> x0, blocking collectives: 14.9 us -> none
    dot_general x1 -> x0, matrix products: 7.54 us -> none  [body(): jnp.dot(scaled, head_weight, preferred_element_type=jnp.float32)]
    all_to_all x1, starting transfers between devices: 11.1 us -> 5.53 us  [tail(): lax.all_to_all(outgoing, 'vocab', split_axis=0, concat_axis=0, tiled=True)]
  transfers between devices with their start and end apart: 4 -> 1, of which waited for: 4 -> 1; matrix products, arithmetic and copies ran while one was open for 2% -> 0% of each run, Pallas kernels for 0% -> 0%
where the time goes in v2:
time: 158 us
  Pallas kernels  118 us (75%)
  waiting for transfers between devices  19.7 us (12%)
  local copies, waits for them, and re-layouts  8.69 us (6%)
  starting transfers between devices  5.53 us (4%)
  other arithmetic  5.17 us (3%)
    pallas_call x1, Pallas kernels, head(): pl.pallas_call(head_kernel, out_shape=[jax.ShapeDtypeStruct((group, colum...  118 us
    all_to_all x1, waiting for transfers between devices, tail(): lax.all_to_all(outgoing, 'vocab', split_axis=0, concat_axis=0, tiled=True)  19.7 us
    all_to_all x1, starting transfers between devices, tail(): lax.all_to_all(outgoing, 'vocab', split_axis=0, concat_axis=0, tiled=True)  5.53 us
    unnamed x16, local copies, waits for them, and re-layouts  4.5 us
  transfers between devices with their start and end apart: 1, of which 1 were waited for; matrix products, arithmetic and copies ran while one was open for 0% of the time, Pallas kernels for 0%

profile of v2, /device:TPU:1, one launch (start us, length us, event | category | flops | bytes accessed | tf_op | source)
XLA Modules:
  0.0 157.8 jit_solution(18056692543092193012)
XLA Ops:
  0.0 1.0 select_subtract_fusion
  1.0 0.3 fusion
  1.3 0.1 select_reduce_fusion
  1.5 0.0 copy-start
  1.5 1.9 %copy-done = bf16[1024,1536]{1,0:T(8,128)(2,1)S(1)} copy-done((bf16[1024,1536]{1,0:T(8,128)(2,1)S(1)}, bf16[1024,1536]{1,0:T(8,128)(2,1)}, u32[]{:S(2)}) %copy-start) | copy-done | bytes 3145752
  3.4 0.0 copy-start.1
  3.4 1.0 copy-done.1
  4.5 0.0 copy-start.2
  4.5 0.8 copy-done.2
  5.2 0.0 copy-start.3
  5.2 0.7 copy-done.3
  5.9 0.0 copy-start.6
  5.9 118.1 %shard_map.73 = (f32[128,1536]{1,0:T(8,128)S(1)}, f32[8,128]{1,0:T(8,128)S(1)}) custom-call(f32[1,16,8192]{2,1,0:T(8,128)S(1)} %copy-done.1, bf16[16,1024]{1,0:T(8,128)(2,1)S(1)} %copy-done.2, f32[1,1024]{1,0:T(1,128)S(1)} %bitcast.113, bf16[1024,1536]{1,0:T(8,128)(2,1)S(1)} %copy-done), custom_call_target="tpu_custom_call" | custom-call | tf_op jit(solution)/shard_map/pallas_call | solution.py:305
  124.0 0.0 copy-done.6
  124.0 0.1 convert_reduce_fusion
  124.1 0.2 fusion.14
  124.3 0.3 exponential_reduce_fusion
  124.6 0.3 select_dynamic-update-slice_fusion.4
  124.9 0.3 select_dynamic-update-slice_fusion.3
  125.1 0.3 select_dynamic-update-slice_fusion.2
  125.4 0.3 select_dynamic-update-slice_fusion.1
  125.7 0.1 select_dynamic-update-slice_fusion
  125.8 0.0 copy-start.5
  125.8 0.0 copy-start.4
  125.8 0.4 fusion.1
  126.3 1.0 reshape.107
  127.3 5.5 %all-to-all-start = ((f32[64,4,640]{2,1,0:T(4,128)}), f32[64,4,640]{2,1,0:T(4,128)S(1)}, u32[]{:S(2)}, u32[]{:S(2)}) async-start(f32[64,4,640]{2,1,0:T(4,128)} %reshape.107), calls=%async_computation | async-start | bytes 1310720 | tf_op jit(solution)/shard_map/all_to_all | solution.py:67
  132.9 0.0 copy-done.5
  132.9 0.1 select_reduce_fusion.1
  133.0 0.0 copy-done.4
  133.0 0.1 multiply_reduce_fusion
  133.2 0.1 compare_and_fusion
  133.3 19.7 %all-to-all-done = f32[64,4,640]{2,1,0:T(4,128)S(1)} async-done(((f32[64,4,640]{2,1,0:T(4,128)}), f32[64,4,640]{2,1,0:T(4,128)S(1)}, u32[]{:S(2)}, u32[]{:S(2)}) %all-to-all-start) | async-done | bytes 655392 | tf_op jit(solution)/shard_map/all_to_all | solution.py:67
  152.9 0.2 fusion.15
  153.1 0.1 copy.17
  153.2 0.1 copy.18
  153.3 0.2 fusion.11
  153.6 0.3 reshape.108
  153.8 2.8 %gather_fusion = f32[1024,128]{1,0:T(8,128)S(1)} fusion(f32[1280,128]{1,0:T(8,128)S(1)} %reshape.108, s32[1024]{0:T(1024)S(1)} %broadcast_clamp_fusion), kind=kCustom, calls=%fused_computation | custom fusion | bytes 1052672 | tf_op jit(solution)/shard_map/jit(_take)/gather | solution.py:74
  156.7 1.1 subtract_select_fusion
  (15 shorter events, 0.1 us)
Async XLA Ops:
  1.5 1.9 %copy-start = (bf16[1024,1536]{1,0:T(8,128)(2,1)S(1)}, bf16[1024,1536]{1,0:T(8,128)(2,1)}, u32[]{:S(2)}) copy-start(bf16[1024,1536]{1,0:T(8,128)(2,1)} %w_hbm.1) | copy-start | bytes 9437188
  3.4 1.0 copy-start.1
  4.5 0.8 copy-start.2
  5.2 0.7 copy-start.3
  5.9 118.1 %copy-start.6 = (s32[128]{0:T(128)S(1)}, s32[128]{0:T(128)}, u32[]{:S(2)}) copy-start(s32[128]{0:T(128)} %param.11) | copy-start | bytes 1540
  125.8 7.0 %copy-start.5 = (s32[128]{0:T(128)S(1)}, s32[128]{0:T(128)}, u32[]{:S(2)}) copy-start(s32[128]{0:T(128)} %param.13) | copy-start | bytes 1540
  125.8 7.2 %copy-start.4 = (s32[128,256]{1,0:T(8,128)S(1)}, s32[128,256]{1,0:T(8,128)}, u32[]{:S(2)}) copy-start(s32[128,256]{1,0:T(8,128)} %param.12) | copy-start | bytes 393220
  127.3 25.6 %all-to-all-start = ((f32[64,4,640]{2,1,0:T(4,128)}), f32[64,4,640]{2,1,0:T(4,128)S(1)}, u32[]{:S(2)}, u32[]{:S(2)}) async-start(f32[64,4,640]{2,1,0:T(4,128)} %reshape.107), calls=%async_computation | async-start | bytes 1310720 | tf_op jit(solution)/shard_map/all_to_all | solution.py:67

commit v3 on v2

--- a/solution.py
+++ b/solution.py
@@ -80,9 +80,9 @@
 
 
 def head_kernel(
-    part_ref, res_ref, gain_ref, w_hbm, raw_ref, sq_ref,
-    w, rs_in, rows, scaled, col, sq_part, sq_in, ring, term,
-    w_sem, rs_s, rs_r, ag_s, ag_r, ring_s, ring_r, sq_s, sq_r,
+    part_hbm, res_hbm, gain_hbm, w_hbm, raw_ref, sq_ref,
+    w, part, res, gain, rs_in, rows, scaled, col, sq_part, sq_in, ring, term,
+    in_sem, rs_s, rs_r, ag_s, ag_r, ring_s, ring_r, sq_s, sq_r,
 ):
     y = lax.axis_index("tp")
     v = lax.axis_index("vocab")
@@ -90,9 +90,10 @@
     z = lax.rem(lax.div(v, 2), N_Z)
     x = lax.div(v, 2 * N_Z)
     turn = 1 - 2 * core
-    local_rows, share = res_ref.shape
-    half = share // 2
+    local_rows, share = res.shape
+    few = local_rows // 2
     group = N_Y * local_rows
+    half = group // 2
 
     def at_x(q):
         return lax.rem(x - turn * q + N_X, N_X)
@@ -106,8 +107,17 @@
     def along_tp(d):
         return (lax.rem(y + d + N_Y, N_Y), v)
 
-    weight_copy = pltpu.make_async_copy(w_hbm, w, w_sem)
-    weight_copy.start()
+    def columns_of(at):
+        return pl.ds(pl.multiple_of(at * share, share), share)
+
+    loads = [
+        pltpu.make_async_copy(part_hbm.at[0, :, columns_of(y)], part, in_sem.at[0]),
+        pltpu.make_async_copy(res_hbm, res, in_sem.at[1]),
+        pltpu.make_async_copy(gain_hbm, gain, in_sem.at[2]),
+        pltpu.make_async_copy(w_hbm, w, in_sem.at[3]),
+    ]
+    for load in loads:
+        load.start()
 
     peers = [along_tp(d) for d in range(1, N_Y)]
     peers += [device(-1, 0, core), device(1, 0, core), device(0, -1, core), device(0, 1, core)]
@@ -123,22 +133,27 @@
             device_id=peer, device_id_type=pl.DeviceIdType.MESH,
         )
 
-    first = []
-    for d in (1, 7, 2, 6, 3, 5, 4):
-        to = lax.rem(y + d, N_Y)
-        source = part_ref.at[0, :, pl.ds(pl.multiple_of(to * share, share), share)]
-        copy = remote(source, rs_in.at[d - 1], rs_s.at[d - 1], rs_r.at[d - 1], along_tp(d))
-        copy.start()
-        first.append(copy)
-    mixed = part_ref[0, :, pl.ds(pl.multiple_of(y * share, share), share)]
-    mixed = mixed + res_ref[...].astype(jnp.float32)
-    for copy in first:
-        copy.wait_recv()
-    for d in range(1, N_Y):
-        mixed = mixed + rs_in[d - 1]
+    first = {}
+    for h in range(2):
+        for d in (4, 1, 7, 2, 6, 3, 5):
+            source = part_hbm.at[0, pl.ds(h * few, few), columns_of(lax.rem(y + d, N_Y))]
+            copy = remote(
+                source, rs_in.at[h, d - 1], rs_s.at[h, d - 1], rs_r.at[h, d - 1], along_tp(d)
+            )
+            copy.start()
+            first[h, d] = copy
+    for load in loads[:3]:
+        load.wait()
     own = x * N_Z + z
-    rows[0, core, own] = mixed[:, :half]
-    rows[1, core, own] = mixed[:, half:]
+
+    def mix(h):
+        at = slice(h * few, (h + 1) * few)
+        mixed = part[at] + res[...].astype(jnp.float32)[at]
+        for d in range(1, N_Y):
+            first[h, d].wait_recv()
+        for d in range(1, N_Y):
+            mixed = mixed + rs_in[h, d - 1]
+        rows[h, core, own] = mixed
 
     limits = {"z": (N_Z // 2, N_Z // 2 - 1), "x": (N_X // 2, N_X // 2 - 1)}
     places = [
@@ -194,31 +209,29 @@
     def order(place):
         h, p, q = place
         main, other = (p, q) if h == 0 else (q, p)
-        return (abs(p) + abs(q), abs(other), h, main)
-
-    for h, p, q in sorted(places, key=order):
-        if (p, q) != (0, 0):
+        return (abs(p) + abs(q) + 2 * h, abs(other), h, main)
+
+    def wait_siblings(h):
+        for _, p, q in sorted((place for place in places if place[0] == h), key=order):
             i = ids[(h, p, q)]
-            block = held(h, p, q)
-            remote(block, block, ag_s.at[0, i], ag_r.at[0, i], device(0, 0, 1 - core)).wait_recv()
-        arrived(h, p, q)
-    for h, p, q in sorted(places, key=order):
-        i = ids[(h, p, q)]
-        block = rows.at[h, 1 - core, at_x(-q) * N_Z + at_z(-p)]
-        remote(block, block, ag_s.at[1, i], ag_r.at[1, i], device(0, 0, 1 - core)).wait_recv()
-
-    def prepare(g):
+            block = rows.at[h, 1 - core, at_x(-q) * N_Z + at_z(-p)]
+            remote(block, block, ag_s.at[1, i], ag_r.at[1, i], device(0, 0, 1 - core)).wait_recv()
+
+    def prepare(g, h):
+        for b in range(N_Y // 2):
+            at = lax.div(g * N_Y, 2) + b
+            pair = jnp.concatenate([rows[h, 0, at], rows[h, 1, at]], axis=0) * gain[...]
+            start = pl.multiple_of(g * group + h * half + b * local_rows, local_rows)
+            scaled[pl.ds(start, local_rows), :] = pair.astype(jnp.bfloat16)
+
+    def square(g):
         for b in range(N_Y):
             at = lax.div(g * N_Y, 2) + b // 2
-            low = rows[0, b % 2, at]
-            high = rows[1, b % 2, at]
-            start = pl.multiple_of(g * group + b * local_rows, local_rows)
-            scaled[pl.ds(start, local_rows), :half] = (low * gain_ref[:, :half]).astype(jnp.bfloat16)
-            scaled[pl.ds(start, local_rows), half:] = (high * gain_ref[:, half:]).astype(jnp.bfloat16)
-            squares = jnp.sum(low * low + high * high, axis=1, keepdims=True)
-            col[b * local_rows : (b + 1) * local_rows, :] = jnp.broadcast_to(
-                squares, (local_rows, BLOCK)
-            )
+            for h in range(2):
+                block = rows[h, b % 2, at]
+                squares = jnp.sum(block * block, axis=1, keepdims=True)
+                start = b * local_rows + h * few
+                col[start : start + few, :] = jnp.broadcast_to(squares, (few, BLOCK))
         sq_part[g] = jnp.transpose(col[...])[:8]
 
     width = ring.shape[-1]
@@ -231,24 +244,55 @@
     def group_at(way, s):
         return lax.rem(y + N_Y - 1 - s, N_Y) if way == 0 else lax.rem(y + 1 + s, N_Y)
 
-    def hop(way, s, j):
+    def hop(way, s, j, h):
+        at = pl.ds(h * half, half)
         return remote(
-            ring.at[way, s, j], ring.at[way, s + 1, j], ring_s.at[way, s, j], ring_r.at[way, s, j],
+            ring.at[way, s, j, at], ring.at[way, s + 1, j, at],
+            ring_s.at[way, s, j, h], ring_r.at[way, s, j, h],
             along_tp(1 if way == 0 else -1),
         )
 
-    weight_copy.wait()
-    for way in range(2):
-        prepare(group_at(way, 0))
-        for j in range(SUBS):
-            ring[way, 0, j] = own_term(group_at(way, 0), way, j)
-            hop(way, 0, j).start()
+    def begin(h):
+        for way in range(2):
+            g = group_at(way, 0)
+            prepare(g, h)
+            left = scaled[pl.ds(pl.multiple_of(g * group + h * half, half), half), :]
+            for j in range(SUBS):
+                start = (way * SUBS + j) * width
+                ring[way, 0, j, h * half : (h + 1) * half] = jnp.dot(
+                    left, w[:, start : start + width], preferred_element_type=jnp.float32
+                )
+                hop(way, 0, j, h).start()
+
+    mix(0)
+    waiting = sorted(places, key=order)
+    for place in waiting:
+        h, p, q = place
+        if (p, q) == (0, 0):
+            if h == 1:
+                mix(1)
+        else:
+            i = ids[place]
+            block = held(h, p, q)
+            remote(block, block, ag_s.at[0, i], ag_r.at[0, i], device(0, 0, 1 - core)).wait_recv()
+        arrived(h, p, q)
+        if place == [other for other in waiting if other[0] == 0][-1]:
+            wait_siblings(0)
+            loads[3].wait()
+            begin(0)
+    wait_siblings(1)
+    begin(1)
 
     @pl.loop(2, N_Y + 1)
     def _(k):
         @pl.when(k != N_Y - 1)
         def _():
-            prepare(lax.rem(y + k, N_Y))
+            for h in range(2):
+                prepare(lax.rem(y + k, N_Y), h)
+
+    @pl.loop(0, N_Y)
+    def _(g):
+        square(g)
 
     squares_out = []
     for d in range(1, N_Y):
@@ -262,11 +306,13 @@
         for way in range(2):
             for j in range(SUBS):
                 term[way, j] = own_term(group_at(way, s), way, j)
-        for j in range(SUBS):
-            for way in range(2):
-                hop(way, s - 1, j).wait_recv()
-                ring[way, s, j] = ring[way, s, j] + term[way, j]
-                hop(way, s, j).start()
+        for h in range(2):
+            at = slice(h * half, (h + 1) * half)
+            for j in range(SUBS):
+                for way in range(2):
+                    hop(way, s - 1, j, h).wait_recv()
+                    ring[way, s, j, at] = ring[way, s, j, at] + term[way, j, at]
+                    hop(way, s, j, h).start()
 
     for way in range(2):
         for j in range(SUBS):
@@ -277,20 +323,25 @@
     for d in range(1, N_Y):
         total = total + sq_in[d - 1]
     sq_ref[...] = total
-    for j in range(SUBS):
-        for way in range(2):
-            hop(way, N_Y - 2, j).wait_recv()
-            start = (way * SUBS + j) * width
-            raw_ref[:, start : start + width] = ring[way, N_Y - 1, j] + term[way, j]
-
-    for copy in first + sent + squares_out:
+    for h in range(2):
+        for j in range(SUBS):
+            for way in range(2):
+                hop(way, N_Y - 2, j, h).wait_recv()
+                start = (way * SUBS + j) * width
+                for b in range(N_Y):
+                    at = slice(h * half + b * few, h * half + (b + 1) * few)
+                    to = slice(b * local_rows + h * few, b * local_rows + (h + 1) * few)
+                    raw_ref[to, start : start + width] = ring[way, N_Y - 1, j, at] + term[way, j, at]
+
+    for copy in list(first.values()) + sent + squares_out:
         copy.wait_send()
 
     @pl.loop(0, N_Y - 1)
     def _(s):
         for way in range(2):
             for j in range(SUBS):
-                hop(way, s, j).wait_send()
+                for h in range(2):
+                    hop(way, s, j, h).wait_send()
 
 
 def head(partials, residual, norm_gain, head_weight):
@@ -308,30 +359,33 @@
             jax.ShapeDtypeStruct((group, columns), f32),
             jax.ShapeDtypeStruct((8, BLOCK), f32),
         ],
-        in_specs=[vmem, vmem, vmem, pl.BlockSpec(memory_space=pl.ANY)],
+        in_specs=[pl.BlockSpec(memory_space=pl.ANY)] * 4,
         out_specs=[vmem, vmem],
         scratch_shapes=[
             pltpu.VMEM((share, columns), jnp.bfloat16),
-            pltpu.VMEM((N_Y - 1, local_rows, share), f32),
-            pltpu.VMEM((2, 2, chips, local_rows, share // 2), f32),
+            pltpu.VMEM((local_rows, share), f32),
+            pltpu.VMEM((local_rows, share), residual.dtype),
+            pltpu.VMEM((1, share), f32),
+            pltpu.VMEM((2, N_Y - 1, local_rows // 2, share), f32),
+            pltpu.VMEM((2, 2, chips, local_rows // 2, share), f32),
             pltpu.VMEM((2 * chips * local_rows, share), jnp.bfloat16),
             pltpu.VMEM((group, BLOCK), f32),
             pltpu.VMEM((N_Y, 8, BLOCK), f32),
             pltpu.VMEM((N_Y - 1, 8, BLOCK), f32),
             pltpu.VMEM((2, N_Y, SUBS, group, width), f32),
             pltpu.VMEM((2, SUBS, group, width), f32),
-            dma,
-            dma((N_Y - 1,)),
-            dma((N_Y - 1,)),
+            dma((4,)),
+            dma((2, N_Y - 1)),
+            dma((2, N_Y - 1)),
             dma((2, 2 * chips)),
             dma((2, 2 * chips)),
-            dma((2, N_Y - 1, SUBS)),
-            dma((2, N_Y - 1, SUBS)),
+            dma((2, N_Y - 1, SUBS, 2)),
+            dma((2, N_Y - 1, SUBS, 2)),
             dma((N_Y - 1,)),
             dma((N_Y - 1,)),
         ],
         compiler_params=pltpu.CompilerParams(
-            collective_id=0, has_side_effects=True, vmem_limit_bytes=48 << 20
+            collective_id=0, has_side_effects=True, vmem_limit_bytes=63 << 20
         ),
     )(partials, residual, norm_gain.reshape(1, share), head_weight)
     return raw, squares[0]

time: 158 us -> 156 us (0.987)
  local copies, waits for them, and re-layouts: 8.69 us -> 4.33 us
  other arithmetic: 5.17 us -> 6.98 us
    unnamed x16 -> x8, local copies, waits for them, and re-layouts: 4.5 us -> 0.13 us
where the time goes in v3:
time: 156 us
  Pallas kernels  118 us (76%)
  waiting for transfers between devices  19.7 us (13%)
  other arithmetic  6.98 us (4%)
  starting transfers between devices  6.36 us (4%)
  local copies, waits for them, and re-layouts  4.33 us (3%)
    pallas_call x1, Pallas kernels, head(): pl.pallas_call(head_kernel, out_shape=[jax.ShapeDtypeStruct((group, colum...  118 us
    all_to_all x1, waiting for transfers between devices, tail(): lax.all_to_all(outgoing, 'vocab', split_axis=0, concat_axis=0, tiled=True)  19.7 us
    all_to_all x1, starting transfers between devices, tail(): lax.all_to_all(outgoing, 'vocab', split_axis=0, concat_axis=0, tiled=True)  6.36 us
  transfers between devices with their start and end apart: 1, of which 1 were waited for; matrix products, arithmetic and copies ran while one was open for 0% of the time, Pallas kernels for 0%

profile of v3, /device:TPU:1, one launch (start us, length us, event | category | flops | bytes accessed | tf_op | source)
XLA Modules:
  0.0 155.8 jit_solution(16503018703787902333)
XLA Ops:
  0.0 1.0 select_subtract_fusion
  1.0 0.3 fusion
  1.3 0.1 select_reduce_fusion
  1.5 0.0 copy-start.2
  1.5 117.8 %shard_map.73 = (f32[128,1536]{1,0:T(8,128)}, f32[8,128]{1,0:T(8,128)}) custom-call(f32[1,16,8192]{2,1,0:T(8,128)} %part_hbm.1, bf16[16,1024]{1,0:T(8,128)(2,1)} %res_hbm.1, f32[1,1024]{1,0:T(1,128)} %bitcast.116, bf16[1024,1536]{1,0:T(8,128)(2,1)} %w_hbm.1), custom_call_target="tpu_custom_call" | custom-call | tf_op jit(solution)/shard_map/pallas_call | solution.py:356
  119.3 0.7 rsqrt_bitcast_fusion
  120.0 0.0 copy-done.2
  120.0 0.1 convert_reduce_fusion
  120.1 1.3 fusion.14
  121.4 0.3 exponential_reduce_fusion
  121.7 0.3 select_dynamic-update-slice_fusion.4
  122.0 0.3 select_dynamic-update-slice_fusion.3
  122.3 0.3 select_dynamic-update-slice_fusion.2
  122.6 0.3 select_dynamic-update-slice_fusion.1
  122.8 0.1 select_dynamic-update-slice_fusion
  122.9 0.0 copy-start.1
  123.0 0.0 copy-start
  123.0 0.4 fusion.1
  123.4 1.0 reshape.107
  124.4 6.4 %all-to-all-start = ((f32[64,4,640]{2,1,0:T(4,128)}), f32[64,4,640]{2,1,0:T(4,128)S(1)}, u32[]{:S(2)}, u32[]{:S(2)}) async-start(f32[64,4,640]{2,1,0:T(4,128)} %reshape.107), calls=%async_computation | async-start | bytes 1310720 | tf_op jit(solution)/shard_map/all_to_all | solution.py:67
  130.8 0.0 copy-done.1
  130.8 0.1 select_reduce_fusion.1
  130.9 0.0 copy-done
  131.0 0.1 multiply_reduce_fusion
  131.1 0.1 compare_and_fusion
  131.2 19.7 %all-to-all-done = f32[64,4,640]{2,1,0:T(4,128)S(1)} async-done(((f32[64,4,640]{2,1,0:T(4,128)}), f32[64,4,640]{2,1,0:T(4,128)S(1)}, u32[]{:S(2)}, u32[]{:S(2)}) %all-to-all-start) | async-done | bytes 655392 | tf_op jit(solution)/shard_map/all_to_all | solution.py:67
  150.9 0.2 fusion.15
  151.1 0.1 copy.17
  151.2 0.1 copy.18
  151.3 0.2 fusion.11
  151.5 0.3 reshape.108
  151.8 2.8 %gather_fusion = f32[1024,128]{1,0:T(8,128)S(1)} fusion(f32[1280,128]{1,0:T(8,128)S(1)} %reshape.108, s32[1024]{0:T(1024)S(1)} %broadcast_clamp_fusion), kind=kCustom, calls=%fused_computation | custom fusion | bytes 1052672 | tf_op jit(solution)/shard_map/jit(_take)/gather | solution.py:74
  154.6 1.1 subtract_select_fusion
  (14 shorter events, 0.1 us)
Async XLA Ops:
  1.5 118.5 %copy-start.2 = (s32[128]{0:T(128)S(1)}, s32[128]{0:T(128)}, u32[]{:S(2)}) copy-start(s32[128]{0:T(128)} %param.11) | copy-start | bytes 1540
  122.9 7.9 %copy-start.1 = (s32[128]{0:T(128)S(1)}, s32[128]{0:T(128)}, u32[]{:S(2)}) copy-start(s32[128]{0:T(128)} %param.13) | copy-start | bytes 1540
  123.0 8.0 %copy-start = (s32[128,256]{1,0:T(8,128)S(1)}, s32[128,256]{1,0:T(8,128)}, u32[]{:S(2)}) copy-start(s32[128,256]{1,0:T(8,128)} %param.12) | copy-start | bytes 393220
  124.4 26.5 %all-to-all-start = ((f32[64,4,640]{2,1,0:T(4,128)}), f32[64,4,640]{2,1,0:T(4,128)S(1)}, u32[]{:S(2)}, u32[]{:S(2)}) async-start(f32[64,4,640]{2,1,0:T(4,128)} %reshape.107), calls=%async_computation | async-start | bytes 1310720 | tf_op jit(solution)/shard_map/all_to_all | solution.py:67

commit v4 on v3

--- a/solution.py
+++ b/solution.py
@@ -77,6 +77,7 @@
 
 N_Y, N_X, N_Z = 8, 4, 8
 SUBS = 3
+LAG = 3
 
 
 def head_kernel(
@@ -163,7 +164,6 @@
         for q in range(-limits["x"][1], limits["x"][0] + 1)
     ]
     ids = {place: i for i, place in enumerate(places)}
-    sent = []
 
     def held(h, p, q):
         return rows.at[h, core, at_x(q) * N_Z + at_z(p)]
@@ -171,17 +171,13 @@
     def pass_on(h, p, q, new_p, new_q):
         peer = device(p - new_p, q - new_q, core)
         i = ids[(h, new_p, new_q)]
-        copy = remote(held(h, p, q), held(h, p, q), ag_s.at[0, i], ag_r.at[0, i], peer)
-        copy.start()
-        sent.append(copy)
+        remote(held(h, p, q), held(h, p, q), ag_s.at[0, i], ag_r.at[0, i], peer).start()
 
     def to_sibling(h, p, q):
         i = ids[(h, p, q)]
-        copy = remote(
+        remote(
             held(h, p, q), held(h, p, q), ag_s.at[1, i], ag_r.at[1, i], device(0, 0, 1 - core)
-        )
-        copy.start()
-        sent.append(copy)
+        ).start()
 
     def along_z(h, p, q):
         if 0 <= p < limits["z"][0]:
@@ -195,8 +191,8 @@
         if -limits["x"][1] < q <= 0:
             pass_on(h, p, q, p, q - 1)
 
-    def arrived(h, p, q):
-        if h == 0:
+    def arrived(z_first, h, p, q):
+        if z_first:
             if q == 0:
                 along_z(h, p, q)
             along_x(h, p, q)
@@ -206,16 +202,44 @@
             along_z(h, p, q)
         to_sibling(h, p, q)
 
-    def order(place):
-        h, p, q = place
-        main, other = (p, q) if h == 0 else (q, p)
-        return (abs(p) + abs(q) + 2 * h, abs(other), h, main)
+    def plan(flip):
+        def key(place):
+            h, p, q = place
+            main, other = (p, q) if h == flip else (q, p)
+            return (abs(p) + abs(q) + LAG * h, h, abs(other), main)
+
+        filled = sorted(places, key=key)
+        last = max(k for k, place in enumerate(filled) if place[0] == 0)
+        return filled[: last + 1], filled[last + 1 :]
+
+    def gather(flip, some):
+        for h, p, q in some:
+            if (p, q) == (0, 0):
+                if h == 1:
+                    mix(1)
+            else:
+                i = ids[(h, p, q)]
+                block = held(h, p, q)
+                remote(
+                    block, block, ag_s.at[0, i], ag_r.at[0, i], device(0, 0, 1 - core)
+                ).wait_recv()
+            arrived(h == flip, h, p, q)
+
+    def on_each_core(part):
+        for flip in range(2):
+
+            @pl.when(core == flip)
+            def _():
+                gather(flip, plan(flip)[part])
 
     def wait_siblings(h):
-        for _, p, q in sorted((place for place in places if place[0] == h), key=order):
-            i = ids[(h, p, q)]
-            block = rows.at[h, 1 - core, at_x(-q) * N_Z + at_z(-p)]
-            remote(block, block, ag_s.at[1, i], ag_r.at[1, i], device(0, 0, 1 - core)).wait_recv()
+        for place in places:
+            if place[0] == h:
+                i = ids[place]
+                block = rows.at[h, 1 - core, at_x(-place[2]) * N_Z + at_z(-place[1])]
+                remote(
+                    block, block, ag_s.at[1, i], ag_r.at[1, i], device(0, 0, 1 - core)
+                ).wait_recv()
 
     def prepare(g, h):
         for b in range(N_Y // 2):
@@ -265,21 +289,11 @@
                 hop(way, 0, j, h).start()
 
     mix(0)
-    waiting = sorted(places, key=order)
-    for place in waiting:
-        h, p, q = place
-        if (p, q) == (0, 0):
-            if h == 1:
-                mix(1)
-        else:
-            i = ids[place]
-            block = held(h, p, q)
-            remote(block, block, ag_s.at[0, i], ag_r.at[0, i], device(0, 0, 1 - core)).wait_recv()
-        arrived(h, p, q)
-        if place == [other for other in waiting if other[0] == 0][-1]:
-            wait_siblings(0)
-            loads[3].wait()
-            begin(0)
+    on_each_core(0)
+    wait_siblings(0)
+    loads[3].wait()
+    begin(0)
+    on_each_core(1)
     wait_siblings(1)
     begin(1)
 
@@ -333,8 +347,14 @@
                     to = slice(b * local_rows + h * few, b * local_rows + (h + 1) * few)
                     raw_ref[to, start : start + width] = ring[way, N_Y - 1, j, at] + term[way, j, at]
 
-    for copy in list(first.values()) + sent + squares_out:
+    for copy in list(first.values()) + squares_out:
         copy.wait_send()
+    for place in places:
+        i = ids[place]
+        block = rows.at[place[0], core, own]
+        if place[1:] != (0, 0):
+            remote(block, block, ag_s.at[0, i], ag_r.at[0, i], device(0, 0, 1 - core)).wait_send()
+        remote(block, block, ag_s.at[1, i], ag_r.at[1, i], device(0, 0, 1 - core)).wait_send()
 
     @pl.loop(0, N_Y - 1)
     def _(s):

time: 156 us -> 159 us (1.019)
  Pallas kernels: 118 us -> 121 us
    pallas_call x1, Pallas kernels: 118 us -> 121 us  [head(): pl.pallas_call(head_kernel, out_shape=[jax.ShapeDtypeStruct((group, colum...]
where the time goes in v4:
time: 159 us
  Pallas kernels  121 us (76%)
  waiting for transfers between devices  19.7 us (12%)
  other arithmetic  6.98 us (4%)
  starting transfers between devices  6.03 us (4%)
  local copies, waits for them, and re-layouts  4.32 us (3%)
    pallas_call x1, Pallas kernels, head(): pl.pallas_call(head_kernel, out_shape=[jax.ShapeDtypeStruct((group, colum...  121 us
    all_to_all x1, waiting for transfers between devices, tail(): lax.all_to_all(outgoing, 'vocab', split_axis=0, concat_axis=0, tiled=True)  19.7 us
    all_to_all x1, starting transfers between devices, tail(): lax.all_to_all(outgoing, 'vocab', split_axis=0, concat_axis=0, tiled=True)  6.03 us
  transfers between devices with their start and end apart: 1, of which 1 were waited for; matrix products, arithmetic and copies ran while one was open for 0% of the time, Pallas kernels for 0%

profile of v4, /device:TPU:1, one launch (start us, length us, event | category | flops | bytes accessed | tf_op | source)
XLA Modules:
  0.0 158.8 jit_solution(3268304115184824053)
XLA Ops:
  0.0 1.0 select_subtract_fusion
  1.0 0.3 fusion
  1.3 0.1 select_reduce_fusion
  1.5 0.0 copy-start.2
  1.5 121.1 %shard_map.73 = (f32[128,1536]{1,0:T(8,128)}, f32[8,128]{1,0:T(8,128)}) custom-call(f32[1,16,8192]{2,1,0:T(8,128)} %part_hbm.1, bf16[16,1024]{1,0:T(8,128)(2,1)} %res_hbm.1, f32[1,1024]{1,0:T(1,128)} %bitcast.116, bf16[1024,1536]{1,0:T(8,128)(2,1)} %w_hbm.1), custom_call_target="tpu_custom_call" | custom-call | tf_op jit(solution)/shard_map/pallas_call | solution.py:376
  122.7 0.7 rsqrt_bitcast_fusion
  123.4 0.0 copy-done.2
  123.4 0.1 convert_reduce_fusion
  123.5 1.3 fusion.14
  124.8 0.3 exponential_reduce_fusion
  125.1 0.3 select_dynamic-update-slice_fusion.4
  125.4 0.3 select_dynamic-update-slice_fusion.3
  125.6 0.3 select_dynamic-update-slice_fusion.2
  125.9 0.3 select_dynamic-update-slice_fusion.1
  126.2 0.1 select_dynamic-update-slice_fusion
  126.3 0.0 copy-start.1
  126.3 0.0 copy-start
  126.3 0.4 fusion.1
  126.8 1.0 reshape.107
  127.8 6.0 %all-to-all-start = ((f32[64,4,640]{2,1,0:T(4,128)}), f32[64,4,640]{2,1,0:T(4,128)S(1)}, u32[]{:S(2)}, u32[]{:S(2)}) async-start(f32[64,4,640]{2,1,0:T(4,128)} %reshape.107), calls=%async_computation | async-start | bytes 1310720 | tf_op jit(solution)/shard_map/all_to_all | solution.py:67
  133.8 0.0 copy-done.1
  133.9 0.1 select_reduce_fusion.1
  134.0 0.0 copy-done
  134.0 0.1 multiply_reduce_fusion
  134.2 0.1 compare_and_fusion
  134.3 19.7 %all-to-all-done = f32[64,4,640]{2,1,0:T(4,128)S(1)} async-done(((f32[64,4,640]{2,1,0:T(4,128)}), f32[64,4,640]{2,1,0:T(4,128)S(1)}, u32[]{:S(2)}, u32[]{:S(2)}) %all-to-all-start) | async-done | bytes 655392 | tf_op jit(solution)/shard_map/all_to_all | solution.py:67
  153.9 0.2 fusion.15
  154.1 0.1 copy.17
  154.2 0.1 copy.18
  154.3 0.2 fusion.11
  154.6 0.3 reshape.108
  154.8 2.8 %gather_fusion = f32[1024,128]{1,0:T(8,128)S(1)} fusion(f32[1280,128]{1,0:T(8,128)S(1)} %reshape.108, s32[1024]{0:T(1024)S(1)} %broadcast_clamp_fusion), kind=kCustom, calls=%fused_computation | custom fusion | bytes 1052672 | tf_op jit(solution)/shard_map/jit(_take)/gather | solution.py:74
  157.7 1.1 subtract_select_fusion
  (14 shorter events, 0.1 us)
Async XLA Ops:
  1.5 121.8 %copy-start.2 = (s32[128]{0:T(128)S(1)}, s32[128]{0:T(128)}, u32[]{:S(2)}) copy-start(s32[128]{0:T(128)} %param.11) | copy-start | bytes 1540
  126.3 7.5 %copy-start.1 = (s32[128]{0:T(128)S(1)}, s32[128]{0:T(128)}, u32[]{:S(2)}) copy-start(s32[128]{0:T(128)} %param.13) | copy-start | bytes 1540
  126.3 7.7 %copy-start = (s32[128,256]{1,0:T(8,128)S(1)}, s32[128,256]{1,0:T(8,128)}, u32[]{:S(2)}) copy-start(s32[128,256]{1,0:T(8,128)} %param.12) | copy-start | bytes 393220
  127.8 26.1 %all-to-all-start = ((f32[64,4,640]{2,1,0:T(4,128)}), f32[64,4,640]{2,1,0:T(4,128)S(1)}, u32[]{:S(2)}, u32[]{:S(2)}) async-start(f32[64,4,640]{2,1,0:T(4,128)} %reshape.107), calls=%async_computation | async-start | bytes 1310720 | tf_op jit(solution)/shard_map/all_to_all | solution.py:67

commit v5 on v3

--- a/solution.py
+++ b/solution.py
@@ -209,7 +209,7 @@
     def order(place):
         h, p, q = place
         main, other = (p, q) if h == 0 else (q, p)
-        return (abs(p) + abs(q) + 2 * h, abs(other), h, main)
+        return (abs(p) + abs(q) + 3 * h, abs(other), h, main)
 
     def wait_siblings(h):
         for _, p, q in sorted((place for place in places if place[0] == h), key=order):
@@ -236,8 +236,8 @@
 
     width = ring.shape[-1]
 
-    def own_term(g, way, j):
-        left = scaled[pl.ds(pl.multiple_of(g * group, group), group), :]
+    def own_term(g, way, j, h):
+        left = scaled[pl.ds(pl.multiple_of(g * group + h * half, half), half), :]
         start = (way * SUBS + j) * width
         return jnp.dot(left, w[:, start : start + width], preferred_element_type=jnp.float32)
 
@@ -256,12 +256,8 @@
         for way in range(2):
             g = group_at(way, 0)
             prepare(g, h)
-            left = scaled[pl.ds(pl.multiple_of(g * group + h * half, half), half), :]
             for j in range(SUBS):
-                start = (way * SUBS + j) * width
-                ring[way, 0, j, h * half : (h + 1) * half] = jnp.dot(
-                    left, w[:, start : start + width], preferred_element_type=jnp.float32
-                )
+                ring[way, 0, j, h * half : (h + 1) * half] = own_term(g, way, j, h)
                 hop(way, 0, j, h).start()
 
     mix(0)
@@ -280,19 +276,36 @@
             wait_siblings(0)
             loads[3].wait()
             begin(0)
+    def step(s, h, fresh):
+        at = slice(h * half, (h + 1) * half)
+        if fresh:
+            for way in range(2):
+                prepare(group_at(way, s), h)
+        for way in range(2):
+            for j in range(SUBS):
+                term[way, j, at] = own_term(group_at(way, s), way, j, h)
+        for j in range(SUBS):
+            for way in range(2):
+                hop(way, s - 1, j, h).wait_recv()
+                ring[way, s, j, at] = ring[way, s, j, at] + term[way, j, at]
+                hop(way, s, j, h).start()
+
+    step(1, 0, True)
     wait_siblings(1)
     begin(1)
-
-    @pl.loop(2, N_Y + 1)
-    def _(k):
-        @pl.when(k != N_Y - 1)
-        def _():
-            for h in range(2):
-                prepare(lax.rem(y + k, N_Y), h)
-
-    @pl.loop(0, N_Y)
-    def _(g):
-        square(g)
+    step(2, 0, True)
+
+    @pl.loop(1, N_Y // 2)
+    def _(s):
+        step(s, 1, True)
+        step(s + 2, 0, True)
+        square(2 * s - 2)
+        square(2 * s - 1)
+
+    for h in range(2):
+        prepare(y, h)
+    square(N_Y - 2)
+    square(N_Y - 1)
 
     squares_out = []
     for d in range(1, N_Y):
@@ -301,22 +314,18 @@
         copy.start()
         squares_out.append(copy)
 
-    @pl.loop(1, N_Y - 1)
+    @pl.loop(N_Y // 2, N_Y - 1)
     def _(s):
+        step(s, 1, False)
+
+        @pl.when(s + 2 < N_Y - 1)
+        def _():
+            step(s + 2, 0, False)
+
+    for h in range(2):
         for way in range(2):
             for j in range(SUBS):
-                term[way, j] = own_term(group_at(way, s), way, j)
-        for h in range(2):
-            at = slice(h * half, (h + 1) * half)
-            for j in range(SUBS):
-                for way in range(2):
-                    hop(way, s - 1, j, h).wait_recv()
-                    ring[way, s, j, at] = ring[way, s, j, at] + term[way, j, at]
-                    hop(way, s, j, h).start()
-
-    for way in range(2):
-        for j in range(SUBS):
-            term[way, j] = own_term(y, way, j)
+                term[way, j, h * half : (h + 1) * half] = own_term(y, way, j, h)
     for copy in squares_out:
         copy.wait_recv()
     total = sq_part[y]

time: 156 us -> 157 us (level)
  starting transfers between devices: 6.36 us -> 9.06 us
    all_to_all x1, starting transfers between devices: 6.36 us -> 9.06 us  [tail(): lax.all_to_all(outgoing, 'vocab', split_axis=0, concat_axis=0, tiled=True)]
where the time goes in v5:
time: 157 us
  Pallas kernels  117 us (75%)
  waiting for transfers between devices  19.7 us (13%)
  starting transfers between devices  9.06 us (6%)
  other arithmetic  6.98 us (4%)
  local copies, waits for them, and re-layouts  4.32 us (3%)
    pallas_call x1, Pallas kernels, head(): pl.pallas_call(head_kernel, out_shape=[jax.ShapeDtypeStruct((group, colum...  117 us
    all_to_all x1, waiting for transfers between devices, tail(): lax.all_to_all(outgoing, 'vocab', split_axis=0, concat_axis=0, tiled=True)  19.7 us
    all_to_all x1, starting transfers between devices, tail(): lax.all_to_all(outgoing, 'vocab', split_axis=0, concat_axis=0, tiled=True)  9.06 us
  transfers between devices with their start and end apart: 1, of which 1 were waited for; matrix products, arithmetic and copies ran while one was open for 0% of the time, Pallas kernels for 0%

profile of v5, /device:TPU:1, one launch (start us, length us, event | category | flops | bytes accessed | tf_op | source)
XLA Modules:
  0.0 157.2 jit_solution(11543176784372249066)
XLA Ops:
  0.0 1.0 select_subtract_fusion
  1.0 0.3 fusion
  1.3 0.1 select_reduce_fusion
  1.5 0.0 copy-start.2
  1.5 116.5 %shard_map.73 = (f32[128,1536]{1,0:T(8,128)}, f32[8,128]{1,0:T(8,128)}) custom-call(f32[1,16,8192]{2,1,0:T(8,128)} %part_hbm.1, bf16[16,1024]{1,0:T(8,128)(2,1)} %res_hbm.1, f32[1,1024]{1,0:T(1,128)} %bitcast.116, bf16[1024,1536]{1,0:T(8,128)(2,1)} %w_hbm.1), custom_call_target="tpu_custom_call" | custom-call | tf_op jit(solution)/shard_map/pallas_call | solution.py:365
  118.1 0.7 rsqrt_bitcast_fusion
  118.7 0.0 copy-done.2
  118.7 0.1 convert_reduce_fusion
  118.9 1.3 fusion.14
  120.2 0.3 exponential_reduce_fusion
  120.5 0.3 select_dynamic-update-slice_fusion.4
  120.8 0.3 select_dynamic-update-slice_fusion.3
  121.0 0.3 select_dynamic-update-slice_fusion.2
  121.3 0.3 select_dynamic-update-slice_fusion.1
  121.6 0.1 select_dynamic-update-slice_fusion
  121.7 0.0 copy-start.1
  121.7 0.0 copy-start
  121.7 0.4 fusion.1
  122.2 1.0 reshape.107
  123.2 9.1 %all-to-all-start = ((f32[64,4,640]{2,1,0:T(4,128)}), f32[64,4,640]{2,1,0:T(4,128)S(1)}, u32[]{:S(2)}, u32[]{:S(2)}) async-start(f32[64,4,640]{2,1,0:T(4,128)} %reshape.107), calls=%async_computation | async-start | bytes 1310720 | tf_op jit(solution)/shard_map/all_to_all | solution.py:67
  132.3 0.0 copy-done.1
  132.3 0.1 select_reduce_fusion.1
  132.4 0.0 copy-done
  132.4 0.1 multiply_reduce_fusion
  132.6 0.1 compare_and_fusion
  132.7 19.7 %all-to-all-done = f32[64,4,640]{2,1,0:T(4,128)S(1)} async-done(((f32[64,4,640]{2,1,0:T(4,128)}), f32[64,4,640]{2,1,0:T(4,128)S(1)}, u32[]{:S(2)}, u32[]{:S(2)}) %all-to-all-start) | async-done | bytes 655392 | tf_op jit(solution)/shard_map/all_to_all | solution.py:67
  152.3 0.2 fusion.15
  152.6 0.1 copy.17
  152.7 0.1 copy.18
  152.8 0.2 fusion.11
  153.0 0.3 reshape.108
  153.3 2.8 %gather_fusion = f32[1024,128]{1,0:T(8,128)S(1)} fusion(f32[1280,128]{1,0:T(8,128)S(1)} %reshape.108, s32[1024]{0:T(1024)S(1)} %broadcast_clamp_fusion), kind=kCustom, calls=%fused_computation | custom fusion | bytes 1052672 | tf_op jit(solution)/shard_map/jit(_take)/gather | solution.py:74
  156.1 1.1 subtract_select_fusion
  (14 shorter events, 0.1 us)
Async XLA Ops:
  1.5 117.2 %copy-start.2 = (s32[128]{0:T(128)S(1)}, s32[128]{0:T(128)}, u32[]{:S(2)}) copy-start(s32[128]{0:T(128)} %param.11) | copy-start | bytes 1540
  121.7 10.6 %copy-start.1 = (s32[128]{0:T(128)S(1)}, s32[128]{0:T(128)}, u32[]{:S(2)}) copy-start(s32[128]{0:T(128)} %param.13) | copy-start | bytes 1540
  121.7 10.7 %copy-start = (s32[128,256]{1,0:T(8,128)S(1)}, s32[128,256]{1,0:T(8,128)}, u32[]{:S(2)}) copy-start(s32[128,256]{1,0:T(8,128)} %param.12) | copy-start | bytes 393220
  123.2 29.2 %all-to-all-start = ((f32[64,4,640]{2,1,0:T(4,128)}), f32[64,4,640]{2,1,0:T(4,128)S(1)}, u32[]{:S(2)}, u32[]{:S(2)}) async-start(f32[64,4,640]{2,1,0:T(4,128)} %reshape.107), calls=%async_computation | async-start | bytes 1310720 | tf_op jit(solution)/shard_map/all_to_all | solution.py:67
